TPU v7x, 128 devices: a whole 4x4x4 slice. The times are simulated.
128 devices in a mesh: row: 8 (over y, core), col: 16 (over x, z).
Axes of the slice: x: 4, y: 4, z: 4, core: 2. Of those that a mesh axis runs over, the one named last changes fastest.
Arguments:
- points: bfloat16 [1048576, 768], P(('row', 'col')), may hold values from -6 to 6
- node_of_row: int32 [1048576], P(('row', 'col')), may hold values from 0 to 255, as said below
- init_axes: float32 [768, 8], replicated, may hold values from -0.21875 to 0.21875
Outputs:
- projected: float32 [8, 1048576], P(None, ('row', 'col'))
Inputs may be any that keep to these rules, and one draw needn't show every extreme that they name: `node_of_row`: never falls along the points; every one of the 256 nodes has at least 512 points; the points of one device belong to at most 8 nodes, and exactly 8 on some device; a node may cover many devices.
All inputs are finite; a program needn't handle non-finite values.
Results may differ from a plain program's by a relative error of at most 0.0035.
The roundings to bfloat16 on the way count: a program that leaves them out, or rounds other values in their place, can miss the bound.
Values sent between devices are 32-bit elements; how exact they have to be, the bound alone decides.
A program may use at most 128 MiB of HBM per device.

v0:
```python
import jax
import jax.numpy as jnp
from jax import lax
from jax.sharding import Mesh
from jax.sharding import PartitionSpec as P

AXES = 8
ITERS = 3
SPAN_MOST = 8
ROW_COL = ("row_0", "row_1", "col_0", "col_1")


def laid_out(blocks, dim):
    dims = list(blocks.shape[1:])
    dims[dim] *= blocks.shape[0]
    return jnp.moveaxis(blocks, 0, dim).reshape(dims)


def gather_in_order(value, axes, order):
    blocks = value[None]
    for k in order:
        blocks = lax.all_gather(blocks, axes[k], axis=0, tiled=True)
    block = [lax.axis_size(axes[k]) for k in reversed(order)]
    blocks = blocks.reshape(*block, *value.shape)
    turned = sorted(range(len(order)), key=lambda place: order[len(order) - 1 - place])
    return blocks.transpose(*turned, *range(len(order), blocks.ndim)).reshape(-1, *value.shape)


def whole_of(value, axes, order, dim):
    return laid_out(gather_in_order(value, axes, order), dim)


def orthonormal(moment):
    found = []
    for index in range(moment.shape[1]):
        vector = moment[:, index]
        for column in found:
            vector = vector - jnp.sum(column * vector) * column
        vector = vector / jnp.sqrt(jnp.sum(vector * vector))
        found.append(vector)
    return jnp.stack(found, 1)


def lifted_terms(block, frames, centre):
    offset = jnp.einsum("ld,ldk->lk", centre, frames, precision=lax.Precision.HIGHEST)
    flat_frames = frames.astype(jnp.bfloat16).transpose(1, 0, 2).reshape(frames.shape[1], -1)
    spread = jnp.dot(block, flat_frames, preferred_element_type=jnp.float32)
    return spread.reshape(block.shape[0], SPAN_MOST, AXES) - offset[None]


def local_moment(block, member, frames, centre):
    terms = lifted_terms(block, frames, centre)
    lifted = terms.astype(jnp.bfloat16) * member.astype(jnp.bfloat16)[:, :, None]
    moment = lax.dot_general(
        block,
        lifted.reshape(block.shape[0], -1),
        (((0,), (0,)), ((), ())),
        preferred_element_type=jnp.float32,
    )
    moment = moment.reshape(block.shape[1], SPAN_MOST, AXES).transpose(1, 0, 2)
    column_sums = jnp.sum(lifted.astype(jnp.float32), 0)
    return moment - centre[:, :, None] * column_sums[:, None, :]


def settle(pieces, first_node, last_node):
    span_count = last_node - first_node
    first_mark = first_node.astype(jnp.float32)
    last_mark = last_node.astype(jnp.float32)
    flat_parts = [piece.reshape(piece.shape[0], -1) for piece in pieces]
    head_rows = tuple((flat[0:1] for flat in flat_parts))
    tail_rows = tuple((lax.dynamic_slice_in_dim(flat, span_count, 1, 0) for flat in flat_parts))
    tail_only = tuple((jnp.where(span_count > 0, tail, 0.0) for tail in tail_rows))
    node_marks = jnp.stack([first_mark, last_mark]).reshape(1, 2)
    gathered = jax.tree.map(
        lambda part: whole_of(part, ROW_COL, (0, 2, 3, 1), 0), (node_marks,) + head_rows + tail_only
    )
    marks_all = gathered[0]
    count_parts = len(flat_parts)
    not_self = jnp.arange(marks_all.shape[0], dtype=jnp.int32) != lax.axis_index(ROW_COL)
    head_first = (not_self & (marks_all[:, 0] == first_mark))[:, None]
    tail_first = (not_self & (marks_all[:, 1] == first_mark))[:, None]
    head_last = (not_self & (marks_all[:, 0] == last_mark) & (last_node != first_node))[:, None]
    tail_last = (not_self & (marks_all[:, 1] == last_mark) & (last_node != first_node))[:, None]
    into_first = []
    into_last = []
    for index in range(count_parts):
        heads_all = gathered[1 + index]
        tails_all = gathered[1 + count_parts + index]
        into_first.append(
            jnp.sum(
                jnp.where(head_first, heads_all, 0.0) + jnp.where(tail_first, tails_all, 0.0),
                0,
                keepdims=True,
            )
        )
        into_last.append(
            jnp.sum(
                jnp.where(head_last, heads_all, 0.0) + jnp.where(tail_last, tails_all, 0.0),
                0,
                keepdims=True,
            )
        )
    slot_index = jnp.arange(SPAN_MOST, dtype=jnp.int32)[:, None]
    settled = []
    for piece, flat, add_first, add_last in zip(pieces, flat_parts, into_first, into_last):
        whole = (
            flat
            + jnp.where(slot_index == 0, add_first, 0.0)
            + jnp.where(slot_index == span_count, add_last, 0.0)
        )
        settled.append(whole.reshape(piece.shape))
    return settled


def shards(points, node_of_row, init_axes):
    row_count = points.shape[0]
    width = points.shape[1]
    first_node = node_of_row[0]
    last_node = node_of_row[-1]
    slot_index = jnp.arange(SPAN_MOST, dtype=jnp.int32)
    member = (node_of_row[:, None] - first_node == slot_index[None, :]).astype(jnp.float32)
    node_sums = lax.dot_general(
        member.astype(jnp.bfloat16),
        points,
        (((0,), (0,)), ((), ())),
        preferred_element_type=jnp.float32,
    )
    node_counts = jnp.sum(member, 0)
    node_sums, node_counts = settle([node_sums, node_counts], first_node, last_node)
    live_slot = slot_index <= last_node - first_node
    centre = node_sums / jnp.where(live_slot, node_counts, 1.0)[:, None]
    start_frames = jnp.broadcast_to(init_axes, (SPAN_MOST, width, AXES))
    frames = start_frames
    for repeat in range(ITERS):
        moment = local_moment(points, member, frames, centre)
        (moment,) = settle([moment], first_node, last_node)
        moment = jnp.where(live_slot[:, None, None], moment, start_frames)
        frames = jax.vmap(orthonormal)(moment)
    terms = lifted_terms(points, frames, centre)
    coords = jnp.sum(terms * member[:, :, None], 1)
    return coords.reshape(row_count, AXES).T


def solution(mesh):
    split = Mesh(mesh.devices.reshape(4, 2, 4, 4), ("row_0", "row_1", "col_0", "col_1"))
    return jax.shard_map(
        shards,
        mesh=split,
        in_specs=(P(ROW_COL, None), P(ROW_COL), P()),
        out_specs=P(None, ROW_COL),
        check_vma=False,
    )
```

profile of v0, /device:TPU:1, one launch (start us, length us, event | category | flops | bytes accessed | tf_op | source)
XLA Modules:
  0.0 663.2 jit_solution(4486327910379594088)
XLA Ops:
  36.8 10.2 %all_gather.146 = f32[64,1,2]{2,1,0:T(1,128)S(1)} all-gather(f32[16,1,2]{2,1,0:T(1,128)S(1)} %all_gather.145), channel_id=1, replica_groups=mesh['row_0'=4,'row_1'=2,'col_0'=4,'col_1'=4] {'col_1'}, dimensions={0}, use_global_device_ids=true | all-gather | bytes 640 | tf_op jit(solution)/shard_map/all_gather | solution.py:22
  121.5 10.4 %all-gather.8 = f32[128,768]{1,0:T(8,128)S(1)} all-gather(f32[64,768]{1,0:T(8,128)S(1)} %all-gather.7), channel_id=10, replica_groups=mesh['row_0'=4,'row_1'=2,'col_0'=4,'col_1'=4] {'row_1'}, dimensions={0}, use_global_device_ids=true | all-gather | bytes 589824 | tf_op jit(solution)/shard_map/all_gather | solution.py:22
  159.6 10.6 %all-gather.4 = f32[128,768]{1,0:T(8,128)S(1)} all-gather(f32[64,768]{1,0:T(8,128)S(1)} %all-gather.3), channel_id=6, replica_groups=mesh['row_0'=4,'row_1'=2,'col_0'=4,'col_1'=4] {'row_1'}, dimensions={0}, use_global_device_ids=true | all-gather | bytes 589824 | tf_op jit(solution)/shard_map/all_gather | solution.py:22
  202.4 10.8 %all-gather.34 = f32[4,4,6144]{2,1,0:T(4,128)S(1)} all-gather(f32[1,4,6144]{2,1,0:T(4,128)S(1)} %copy.263), channel_id=20, replica_groups=mesh['row_0'=4,'row_1'=2,'col_0'=4,'col_1'=4] {'col_0'}, dimensions={0}, use_global_device_ids=true | all-gather | bytes 491520 | tf_op jit(solution)/shard_map/all_gather | solution.py:22
  223.7 10.9 %all_gather.165 = f32[16,1,6144]{2,1,0:T(1,128)} all-gather(f32[4,1,6144]{2,1,0:T(1,128)S(1)} %all_gather.164), channel_id=1, replica_groups=mesh['row_0'=4,'row_1'=2,'col_0'=4,'col_1'=4] {'col_0'}, dimensions={0}, use_global_device_ids=true | all-gather | bytes 491520 | tf_op jit(solution)/shard_map/all_gather | solution.py:22
  241.7 28.1 %all-gather.52.cloned.1.call-done = f32[64,1,6144]{2,1,0:T(1,128)} async-done(((f32[16,1,6144]{2,1,0:T(1,128)}), f32[64,1,6144]{2,1,0:T(1,128)}) %all-gather.52.cloned.1.call-update) | async-done | bytes 1572880 | tf_op jit(solution)/shard_map/all_gather | solution.py:22
  270.7 16.0 %all-gather.66.cloned.1.call-done = f32[128,6144]{1,0:T(8,128)} async-done(((f32[64,6144]{1,0:T(8,128)}), f32[128,6144]{1,0:T(8,128)}) %all-gather.66.cloned.1.call-update) | async-done | bytes 3145744 | tf_op jit(solution)/shard_map/all_gather | solution.py:22
  291.9 12.6 %all-gather.54.cloned.1.call-done = f32[128,1,6144]{2,1,0:T(1,128)} async-done(((f32[64,1,6144]{2,1,0:T(1,128)}), f32[128,1,6144]{2,1,0:T(1,128)}) %all-gather.54.cloned.1.call-update) | async-done | bytes 3145744 | tf_op jit(solution)/shard_map/all_gather | solution.py:22
  304.4 15.6 %fusion.30 = (f32[6144]{0:T(1024)}, f32[6144]{0:T(1024)}) fusion(f32[2,4,4,4,1,6144]{5,4,3,2,1,0:T(1,128)S(1)} %reshape.2690, pred[4,2,4,4]{0,2,3,1:T(4,128)(4,1)S(1)} %copy.251, f32[4,2,4,4,1,6144]{5,4,0,2,3,1:T(1,128)} %bitcast.468, pred[4,2,4,4]{0,2,3,1:T(4,128)(4,1)S(1)} %copy.249, pred[4,2,4,4]{0,2,3,1:T(4,128)(4,1)S(1)} %copy-done.6, ...), kind=kLoop, calls=%fused_computation.39 | loop fusion | flops 6279168 | bytes 6341120 | tf_op jit(solution)/shard_map/reduce_sum | solution.py:90
  350.3 9.9 %all-gather.35 = f32[4,1,6144]{2,1,0:T(1,128)S(1)} all-gather(f32[1,1,6144]{2,1,0:T(1,128)S(1)} %fusion.57), channel_id=23, replica_groups=mesh['row_0'=4,'row_1'=2,'col_0'=4,'col_1'=4] {'row_0'}, dimensions={0}, use_global_device_ids=true | all-gather | bytes 122880 | tf_op jit(solution)/shard_map/all_gather | solution.py:22
  360.2 10.0 %all-gather.36 = f32[4,4,6144]{2,1,0:T(4,128)S(1)} all-gather(f32[1,4,6144]{2,1,0:T(4,128)S(1)} %copy.274), channel_id=24, replica_groups=mesh['row_0'=4,'row_1'=2,'col_0'=4,'col_1'=4] {'col_0'}, dimensions={0}, use_global_device_ids=true | all-gather | bytes 491520 | tf_op jit(solution)/shard_map/all_gather | solution.py:22
  380.6 11.5 %all_gather.173 = f32[16,1,6144]{2,1,0:T(1,128)} all-gather(f32[4,1,6144]{2,1,0:T(1,128)S(1)} %all_gather.172), channel_id=1, replica_groups=mesh['row_0'=4,'row_1'=2,'col_0'=4,'col_1'=4] {'col_0'}, dimensions={0}, use_global_device_ids=true | all-gather | bytes 491520 | tf_op jit(solution)/shard_map/all_gather | solution.py:22
  392.1 10.7 %all-gather.68.cloned.1.call-done = f32[64,6144]{1,0:T(8,128)} async-done(((f32[16,6144]{1,0:T(8,128)}), f32[64,6144]{1,0:T(8,128)}) %all-gather.68.cloned.1.call-update) | async-done | bytes 1572880 | tf_op jit(solution)/shard_map/all_gather | solution.py:22
  402.9 28.0 %all-gather.56.cloned.1.call-done = f32[64,1,6144]{2,1,0:T(1,128)} async-done(((f32[16,1,6144]{2,1,0:T(1,128)}), f32[64,1,6144]{2,1,0:T(1,128)}) %all-gather.56.cloned.1.call-update) | async-done | bytes 1572880 | tf_op jit(solution)/shard_map/all_gather | solution.py:22
  431.0 16.8 %all-gather.70.cloned.1.call-done = f32[128,6144]{1,0:T(8,128)} async-done(((f32[64,6144]{1,0:T(8,128)}), f32[128,6144]{1,0:T(8,128)}) %all-gather.70.cloned.1.call-update) | async-done | bytes 3145744 | tf_op jit(solution)/shard_map/all_gather | solution.py:22
  452.9 12.7 %all-gather.58.cloned.1.call-done = f32[128,1,6144]{2,1,0:T(1,128)} async-done(((f32[64,1,6144]{2,1,0:T(1,128)}), f32[128,1,6144]{2,1,0:T(1,128)}) %all-gather.58.cloned.1.call-update) | async-done | bytes 3145744 | tf_op jit(solution)/shard_map/all_gather | solution.py:22
  465.6 15.6 %fusion.29 = (f32[6144]{0:T(1024)}, f32[6144]{0:T(1024)}) fusion(f32[2,4,4,4,1,6144]{5,4,3,2,1,0:T(1,128)S(1)} %reshape.2691, pred[4,2,4,4]{0,2,3,1:T(4,128)(4,1)S(1)} %copy.251, f32[4,2,4,4,1,6144]{5,4,0,2,3,1:T(1,128)} %bitcast.470, pred[4,2,4,4]{0,2,3,1:T(4,128)(4,1)S(1)} %copy.249, pred[4,2,4,4]{0,2,3,1:T(4,128)(4,1)S(1)} %copy-done.7, ...), kind=kLoop, calls=%fused_computation.38 | loop fusion | flops 6279168 | bytes 6341120 | tf_op jit(solution)/shard_map/reduce_sum | solution.py:90
  521.1 10.0 %all-gather.38 = f32[4,4,6144]{2,1,0:T(4,128)S(1)} all-gather(f32[1,4,6144]{2,1,0:T(4,128)S(1)} %copy.283), channel_id=28, replica_groups=mesh['row_0'=4,'row_1'=2,'col_0'=4,'col_1'=4] {'col_0'}, dimensions={0}, use_global_device_ids=true | all-gather | bytes 491520 | tf_op jit(solution)/shard_map/all_gather | solution.py:22
  541.5 11.5 %all_gather.181 = f32[16,1,6144]{2,1,0:T(1,128)} all-gather(f32[4,1,6144]{2,1,0:T(1,128)S(1)} %all_gather.180), channel_id=1, replica_groups=mesh['row_0'=4,'row_1'=2,'col_0'=4,'col_1'=4] {'col_0'}, dimensions={0}, use_global_device_ids=true | all-gather | bytes 491520 | tf_op jit(solution)/shard_map/all_gather | solution.py:22
  553.1 10.7 %all-gather.72.cloned.1.call-done = f32[64,6144]{1,0:T(8,128)} async-done(((f32[16,6144]{1,0:T(8,128)}), f32[64,6144]{1,0:T(8,128)}) %all-gather.72.cloned.1.call-update) | async-done | bytes 1572880 | tf_op jit(solution)/shard_map/all_gather | solution.py:22
  563.8 28.0 %all-gather.60.cloned.1.call-done = f32[64,1,6144]{2,1,0:T(1,128)} async-done(((f32[16,1,6144]{2,1,0:T(1,128)}), f32[64,1,6144]{2,1,0:T(1,128)}) %all-gather.60.cloned.1.call-update) | async-done | bytes 1572880 | tf_op jit(solution)/shard_map/all_gather | solution.py:22
  591.8 16.9 %all-gather.74.cloned.1.call-done = f32[128,6144]{1,0:T(8,128)} async-done(((f32[64,6144]{1,0:T(8,128)}), f32[128,6144]{1,0:T(8,128)}) %all-gather.74.cloned.1.call-update) | async-done | bytes 3145744 | tf_op jit(solution)/shard_map/all_gather | solution.py:22
  613.8 12.6 %all-gather.62.cloned.1.call-done = f32[128,1,6144]{2,1,0:T(1,128)} async-done(((f32[64,1,6144]{2,1,0:T(1,128)}), f32[128,1,6144]{2,1,0:T(1,128)}) %all-gather.62.cloned.1.call-update) | async-done | bytes 3145744 | tf_op jit(solution)/shard_map/all_gather | solution.py:22
  626.4 15.0 %fusion.28 = (f32[6144]{0:T(1024)S(1)}, f32[6144]{0:T(1024)S(1)}) fusion(f32[2,4,4,4,1,6144]{5,4,3,2,1,0:T(1,128)S(1)} %reshape.2692, pred[4,2,4,4]{0,2,3,1:T(4,128)(4,1)S(1)} %copy.251, f32[4,2,4,4,1,6144]{5,4,0,2,3,1:T(1,128)} %bitcast.469, pred[4,2,4,4]{0,2,3,1:T(4,128)(4,1)S(1)} %copy.249, pred[4,2,4,4]{0,2,3,1:T(4,128)(4,1)S(1)} %copy-done.8, ...), kind=kLoop, calls=%fused_computation.37 | loop fusion | flops 6279168 | bytes 6341120 | tf_op jit(solution)/shard_map/reduce_sum | solution.py:90
  (314 shorter events, 296.7 us)
Async XLA Ops:
  6.5 235.1 %all-gather.64.cloned.1.call-start = ((), (), s32[]{:S(2)}) async-start(), calls=%async_computation.6 | async-start | bytes 1966080 | tf_op jit(solution)/shard_map/all_gather | solution.py:22
  14.0 161.2 %copy-start.15 = (pred[8]{0:T(512)(128)(4,1)}, pred[8]{0:T(512)(128)(4,1)S(1)}, u32[]{:S(2)}) copy-start(pred[8]{0:T(512)(128)(4,1)S(1)} %iota_compare_fusion.1) | copy-start | bytes 28
  14.0 161.2 %copy-start.17 = (pred[8]{0:T(512)(128)(4,1)}, pred[8]{0:T(512)(128)(4,1)S(1)}, u32[]{:S(2)}) copy-start(pred[8]{0:T(512)(128)(4,1)S(1)} %iota_compare_fusion.3) | copy-start | bytes 28
  93.8 81.5 %copy-start.1 = (f32[768,8]{0,1:T(8,128)S(1)}, f32[768,8]{0,1:T(8,128)}, u32[]{:S(2)}) copy-start(f32[768,8]{0,1:T(8,128)} %param.5) | copy-start | bytes 73732
  189.6 24.6 %slice-start.4 = ((f32[8,768,8]{1,0,2:T(8,128)}), f32[1,768,8]{1,0,2:T(1,128)S(1)}, s32[]{:S(2)}) async-start(f32[8,768,8]{1,0,2:T(8,128)} %bitcast_subtract_fusion.2), calls=%async_computation.16 | async-start | bytes 49152 | tf_op jit(solution)/shard_map/slice | solution.py:70
  214.1 55.7 %all-gather.52.cloned.1.call-start = ((), (), s32[]{:S(2)}) async-start(), calls=%async_computation | async-start | bytes 1966080 | tf_op jit(solution)/shard_map/all_gather | solution.py:22
  234.6 52.1 %all-gather.66.cloned.1.call-start = ((), (), s32[]{:S(2)}) async-start(), calls=%async_computation.7 | async-start | bytes 4718592 | tf_op jit(solution)/shard_map/all_gather | solution.py:22
  241.6 62.8 %all-gather.54.cloned.1.call-start = ((), (), s32[]{:S(2)}) async-start(), calls=%async_computation.1 | async-start | bytes 4718592 | tf_op jit(solution)/shard_map/all_gather | solution.py:22
  269.8 133.0 %all-gather.68.cloned.1.call-start = ((), (), s32[]{:S(2)}) async-start(), calls=%async_computation.8 | async-start | bytes 1966080 | tf_op jit(solution)/shard_map/all_gather | solution.py:22
  270.7 33.8 %copy-start.6 = (pred[4,2,4,4]{0,2,3,1:T(4,128)(4,1)S(1)}, pred[4,2,4,4]{0,2,3,1:T(4,128)(4,1)}, u32[]{:S(2)}) copy-start(pred[4,2,4,4]{0,2,3,1:T(4,128)(4,1)} %copy-done.5) | copy-start | bytes 388
  270.7 33.8 %copy-start.10 = (pred[4,2,4,4]{0,2,3,1:T(4,128)(4,1)S(1)}, pred[4,2,4,4]{0,2,3,1:T(4,128)(4,1)}, u32[]{:S(2)}) copy-start(pred[4,2,4,4]{0,2,3,1:T(4,128)(4,1)} %copy-done.9) | copy-start | bytes 388
  346.6 24.6 %slice-start.5 = ((f32[8,768,8]{1,0,2:T(8,128)}), f32[1,768,8]{1,0,2:T(1,128)S(1)}, s32[]{:S(2)}) async-start(f32[8,768,8]{1,0,2:T(8,128)} %bitcast_subtract_fusion.1), calls=%async_computation.17 | async-start | bytes 49152 | tf_op jit(solution)/shard_map/slice | solution.py:70
  371.1 59.8 %all-gather.56.cloned.1.call-start = ((), (), s32[]{:S(2)}) async-start(), calls=%async_computation.2 | async-start | bytes 1966080 | tf_op jit(solution)/shard_map/all_gather | solution.py:22
  392.1 55.7 %all-gather.70.cloned.1.call-start = ((), (), s32[]{:S(2)}) async-start(), calls=%async_computation.9 | async-start | bytes 4718592 | tf_op jit(solution)/shard_map/all_gather | solution.py:22
  402.8 62.8 %all-gather.58.cloned.1.call-start = ((), (), s32[]{:S(2)}) async-start(), calls=%async_computation.3 | async-start | bytes 4718592 | tf_op jit(solution)/shard_map/all_gather | solution.py:22
  430.9 34.8 %copy-start.7 = (pred[4,2,4,4]{0,2,3,1:T(4,128)(4,1)S(1)}, pred[4,2,4,4]{0,2,3,1:T(4,128)(4,1)}, u32[]{:S(2)}) copy-start(pred[4,2,4,4]{0,2,3,1:T(4,128)(4,1)} %copy-done.5) | copy-start | bytes 388
  430.9 34.7 %copy-start.11 = (pred[4,2,4,4]{0,2,3,1:T(4,128)(4,1)S(1)}, pred[4,2,4,4]{0,2,3,1:T(4,128)(4,1)}, u32[]{:S(2)}) copy-start(pred[4,2,4,4]{0,2,3,1:T(4,128)(4,1)} %copy-done.9) | copy-start | bytes 388
  430.9 132.8 %all-gather.72.cloned.1.call-start = ((), (), s32[]{:S(2)}) async-start(), calls=%async_computation.10 | async-start | bytes 1966080 | tf_op jit(solution)/shard_map/all_gather | solution.py:22
  507.5 24.6 %slice-start.3 = ((f32[8,768,8]{1,0,2:T(8,128)}), f32[1,768,8]{1,0,2:T(1,128)S(1)}, s32[]{:S(2)}) async-start(f32[8,768,8]{1,0,2:T(8,128)} %bitcast_subtract_fusion), calls=%async_computation.15 | async-start | bytes 49152 | tf_op jit(solution)/shard_map/slice | solution.py:70
  532.0 59.8 %all-gather.60.cloned.1.call-start = ((), (), s32[]{:S(2)}) async-start(), calls=%async_computation.4 | async-start | bytes 1966080 | tf_op jit(solution)/shard_map/all_gather | solution.py:22
  553.0 55.7 %all-gather.74.cloned.1.call-start = ((), (), s32[]{:S(2)}) async-start(), calls=%async_computation.11 | async-start | bytes 4718592 | tf_op jit(solution)/shard_map/all_gather | solution.py:22
  563.8 62.7 %all-gather.62.cloned.1.call-start = ((), (), s32[]{:S(2)}) async-start(), calls=%async_computation.5 | async-start | bytes 4718592 | tf_op jit(solution)/shard_map/all_gather | solution.py:22
  591.8 34.6 %copy-start.8 = (pred[4,2,4,4]{0,2,3,1:T(4,128)(4,1)S(1)}, pred[4,2,4,4]{0,2,3,1:T(4,128)(4,1)}, u32[]{:S(2)}) copy-start(pred[4,2,4,4]{0,2,3,1:T(4,128)(4,1)} %copy-done.5) | copy-start | bytes 388
  591.8 34.6 %copy-start.12 = (pred[4,2,4,4]{0,2,3,1:T(4,128)(4,1)S(1)}, pred[4,2,4,4]{0,2,3,1:T(4,128)(4,1)}, u32[]{:S(2)}) copy-start(pred[4,2,4,4]{0,2,3,1:T(4,128)(4,1)} %copy-done.9) | copy-start | bytes 388
  (14 other events, 129.5 us)
Sparse Core Ops, SparseCore 0:
  214.3 27.3 all-gather.63
  243.3 26.4 all-gather.51
  271.5 15.2 all-gather.65
  288.2 16.1 all-gather.53
  371.2 31.5 all-gather.67
  404.3 26.4 all-gather.55
  432.5 15.2 all-gather.69
  449.4 16.1 all-gather.57
  532.1 31.5 all-gather.71
  565.2 26.4 all-gather.59
  593.4 15.2 all-gather.73
  610.2 16.1 all-gather.61
where the time goes:
time: 669 us; the launch traced here: 663 us
  blocking collectives  257 us (38%)
  waiting for transfers between devices  200 us (30%)
  other arithmetic  71.5 us (11%)
  matrix products  59.3 us (9%)
  local copies, waits for them, and re-layouts  52.6 us (8%)
  between operations  21.7 us (3%)
    all_gather x23, blocking collectives, gather_in_order(): blocks = lax.all_gather(blocks, axes[k], axis=0, tiled=True)  225 us
    all_gather x12, waiting for transfers between devices, gather_in_order(): blocks = lax.all_gather(blocks, axes[k], axis=0, tiled=True)  200 us
    reduce_sum x5, other arithmetic, settle(): jnp.sum(jnp.where(head_first, heads_all, 0.0) + jnp.where(tail_first, tai...  47.1 us
    dot_general x4, matrix products, lifted_terms(): spread = jnp.dot(block, flat_frames, preferred_element_type=jnp.float32)  35.1 us
    unnamed x4, blocking collectives  32 us
    reshape x8, local copies, waits for them, and re-layouts, gather_in_order(): blocks = blocks.reshape(*block, *value.shape)  16.1 us
    dot_general x3, matrix products, local_moment(): lax.dot_general(block, lifted.reshape(block.shape[0], -1), (((0,), (0,)),...  16 us
  transfers between devices with their start and end apart: 12, of which 12 were waited for; matrix products, arithmetic and copies ran while one was open for 3% of the time, Pallas kernels for 0%

commit v1 on v0

--- a/solution.py
+++ b/solution.py
@@ -19,7 +19,9 @@
 def gather_in_order(value, axes, order):
     blocks = value[None]
     for k in order:
-        blocks = lax.all_gather(blocks, axes[k], axis=0, tiled=True)
+        blocks = jnp.concatenate(
+            lax.all_to_all(jnp.stack([blocks] * lax.axis_size(axes[k])), axes[k], 0, 0), axis=0
+        )
     block = [lax.axis_size(axes[k]) for k in reversed(order)]
     blocks = blocks.reshape(*block, *value.shape)
     turned = sorted(range(len(order)), key=lambda place: order[len(order) - 1 - place])

time: 669 us -> 631 us (0.943)
  blocking collectives: 257 us -> 13.9 us
  starting transfers between devices: 0.66 us -> 192 us
  local copies, waits for them, and re-layouts: 52.6 us -> 93.4 us
  waiting for transfers between devices: 200 us -> 178 us
  between operations: 21.7 us -> 6.17 us
    all_gather x23 -> x0, blocking collectives: 225 us -> none  [gather_in_order(): blocks = lax.all_gather(blocks, axes[k], axis=0, tiled=True)]
    all_gather x12 -> x0, waiting for transfers between devices: 200 us -> none  [gather_in_order(): blocks = lax.all_gather(blocks, axes[k], axis=0, tiled=True)]
    all_to_all x0 -> x41, starting transfers between devices: none -> 192 us  [gather_in_order(): lax.all_to_all(jnp.stack([blocks] * lax.axis_size(axes[k])), axes[k], 0, 0)]
    all_to_all x0 -> x41, waiting for transfers between devices: none -> 178 us  [gather_in_order(): lax.all_to_all(jnp.stack([blocks] * lax.axis_size(axes[k])), axes[k], 0, 0)]
    unnamed x4 -> x0, blocking collectives: 32 us -> none
    another operation x0 -> x53, local copies, waits for them, and re-layouts: none -> 30.7 us  [the longest x50 30.4 us: gather_in_order(): jnp.stack([blocks] * lax.axis_size(axes[k]))]
    all_to_all x0 -> x13, local copies, waits for them, and re-layouts: none -> 27.6 us  [gather_in_order(): lax.all_to_all(jnp.stack([blocks] * lax.axis_size(axes[k])), axes[k], 0, 0)]
    reduce_sum x5, other arithmetic: 47.1 us -> 24.3 us  [settle(): jnp.sum(jnp.where(head_first, heads_all, 0.0) + jnp.where(tail_first, tai...]
  transfers between devices with their start and end apart: 12 -> 41, of which waited for: 12 -> 33; matrix products, arithmetic and copies ran while one was open for 3% -> 11% of each run, Pallas kernels for 0% -> 0%
where the time goes in v1:
time: 631 us; the launch traced here: 619 us
  starting transfers between devices  192 us (30%)
  waiting for transfers between devices  178 us (28%)
  local copies, waits for them, and re-layouts  93.4 us (15%)
  other arithmetic  71.1 us (11%)
  matrix products  63.7 us (10%)
  blocking collectives  13.9 us (2%)
    all_to_all x41, starting transfers between devices, gather_in_order(): lax.all_to_all(jnp.stack([blocks] * lax.axis_size(axes[k])), axes[k], 0, 0)  192 us
    all_to_all x41, waiting for transfers between devices, gather_in_order(): lax.all_to_all(jnp.stack([blocks] * lax.axis_size(axes[k])), axes[k], 0, 0)  178 us
    dot_general x4, matrix products, lifted_terms(): spread = jnp.dot(block, flat_frames, preferred_element_type=jnp.float32)  34.9 us
    another operation x50, local copies, waits for them, and re-layouts, gather_in_order(): jnp.stack([blocks] * lax.axis_size(axes[k]))  30.4 us
    all_to_all x13, local copies, waits for them, and re-layouts, gather_in_order(): lax.all_to_all(jnp.stack([blocks] * lax.axis_size(axes[k])), axes[k], 0, 0)  27.6 us
    reduce_sum x5, other arithmetic, settle(): jnp.sum(jnp.where(head_first, heads_all, 0.0) + jnp.where(tail_first, tai...  24.3 us
    dot_general x3, matrix products, local_moment(): lax.dot_general(block, lifted.reshape(block.shape[0], -1), (((0,), (0,)),...  20.6 us
    another operation x10, other arithmetic, gather_in_order(): jnp.stack([blocks] * lax.axis_size(axes[k]))  20 us
  transfers between devices with their start and end apart: 41, of which 33 were waited for; matrix products, arithmetic and copies ran while one was open for 11% of the time, Pallas kernels for 0%

profile of v1, /device:TPU:1, one launch (start us, length us, event | category | flops | bytes accessed | tf_op | source)
XLA Modules:
  0.0 618.9 jit_solution(12283485943534989718)
XLA Ops:
  12.2 6.3 %fusion.64 = f32[8,768]{1,0:T(8,128)S(1)} fusion(bf16[8192,768]{1,0:T(8,128)(2,1)} %param.3, s32[8192]{0:T(1024)S(1)} %broadcast_subtract_fusion), kind=kOutput, calls=%fused_computation.340 | convolution fusion | flops 100859904 | bytes 12640256 | tf_op jit(solution)/shard_map/dot_general | solution.py:124
  86.0 14.5 %all-to-all-start.19 = ((f32[2,64,1,1]{1,3,2,0:T(1,128)}), f32[2,64,1,1]{1,3,2,0:T(1,128)S(1)}, u32[]{:S(2)}, u32[]{:S(2)}) async-start(f32[2,64,1,1]{1,3,2,0:T(1,128)} %pad_maximum_fusion.10), calls=%async_computation.19 | async-start | bytes 2048 | tf_op jit(solution)/shard_map/all_to_all | solution.py:23
  108.7 6.5 %all_to_all.234 = f32[4,1,1,768]{3,2,1,0:T(1,128)S(1)} all-to-all(f32[4,1,1,768]{3,2,1,0:T(1,128)S(1)} %stack.206), channel_id=1, replica_groups=mesh['row_0'=4,'row_1'=2,'col_0'=4,'col_1'=4] {'row_0'}, dimensions={0} | all-to-all | bytes 24576 | tf_op jit(solution)/shard_map/all_to_all | solution.py:23
  158.9 10.0 %all-to-all-start.11 = ((f32[2,64,1,768]{3,1,2,0:T(8,128)}), f32[2,64,1,768]{3,1,2,0:T(8,128)S(1)}, u32[]{:S(2)}, u32[]{:S(2)}) async-start(f32[2,64,1,768]{3,1,2,0:T(8,128)} %pad_maximum_fusion.7), calls=%async_computation.11 | async-start | bytes 786432 | tf_op jit(solution)/shard_map/all_to_all | solution.py:23
  177.0 8.6 %convert_reduce_fusion.2 = (f32[8,8]{1,0:T(8,128)S(1)}, bf16[8192,8,8]{0,2,1:T(8,128)(2,1)S(1)}) fusion(bf16[8192,8]{0,1:T(8,128)(2,1)S(1)} %get-tuple-element.187, f32[8,8]{1,0:T(8,128)S(1)} %bitcast.522, bf16[768,8]{0,1:T(8,128)(2,1)S(1)} %convert_element_type.75, bf16[8192,768]{1,0:T(8,128)(2,1)} %param.3), kind=kOutput, calls=%fused_computation.30 | convolution fusion | flops 807927744 | bytes 13775360 | tf_op jit(solution)/shard_map/dot_general | solution.py:49
  185.6 6.8 %convolution_bitcast_fusion.3 = f32[768,8,8]{0,2,1:T(8,128)S(1)} fusion(bf16[8192,768]{1,0:T(8,128)(2,1)} %param.3, bf16[8192,8,8]{0,2,1:T(8,128)(2,1)S(1)} %get-tuple-element.200), kind=kOutput, calls=%fused_computation.34 | convolution fusion | flops 805306368 | bytes 13828096 | tf_op jit(solution)/shard_map/dot_general | solution.py:56
  220.3 6.2 %all-to-all-done.21 = f32[4,4,1,6144]{3,1,2,0:T(4,128)S(1)} async-done(((f32[4,4,1,6144]{3,1,2,0:T(4,128)}), f32[4,4,1,6144]{3,1,2,0:T(4,128)S(1)}, u32[]{:S(2)}, u32[]{:S(2)}) %all-to-all-start.21) | async-done | bytes 393248 | tf_op jit(solution)/shard_map/all_to_all | solution.py:23
  242.0 15.1 %all-to-all-done.22 = f32[4,16,1,6144]{3,1,2,0:T(8,128)S(1)} async-done(((f32[4,16,1,6144]{3,1,2,0:T(8,128)}), f32[4,16,1,6144]{3,1,2,0:T(8,128)S(1)}, u32[]{:S(2)}, u32[]{:S(2)}) %all-to-all-start.22) | async-done | bytes 1572896 | tf_op jit(solution)/shard_map/all_to_all | solution.py:23
  263.9 12.1 %all-to-all-done.26 = f32[4,16,1,6144]{3,1,2,0:T(8,128)S(1)} async-done(((f32[4,16,1,6144]{3,1,2,0:T(8,128)}), f32[4,16,1,6144]{3,1,2,0:T(8,128)S(1)}, u32[]{:S(2)}, u32[]{:S(2)}) %all-to-all-start.26) | async-done | bytes 1572896 | tf_op jit(solution)/shard_map/all_to_all | solution.py:23
  277.1 11.5 %all-to-all-start.23 = ((f32[2,64,1,6144]{3,1,2,0:T(8,128)}), f32[2,64,1,6144]{3,1,2,0:T(8,128)S(1)}, u32[]{:S(2)}, u32[]{:S(2)}) async-start(f32[2,64,1,6144]{3,1,2,0:T(8,128)} %pad_maximum_fusion), calls=%async_computation.23 | async-start | bytes 6291456 | tf_op jit(solution)/shard_map/all_to_all | solution.py:23
  306.4 8.1 %add_reduce_fusion.5 = (f32[6144]{0:T(1024)}, f32[6144]{0:T(1024)}) fusion(f32[4,2,4,4,1,6144]{5,1,0,2,3,4:T(2,128)S(1)} %bitcast.491, f32[4,2,4,4,1,6144]{5,1,0,2,3,4:T(2,128)S(1)} %bitcast.488, pred[4,2,4,4]{1,0,2,3:T(4,128)(4,1)S(1)} %copy-done.19, pred[4,2,4,4]{1,0,2,3:T(4,128)(4,1)S(1)} %copy-done.15, pred[4,2,4,4]{1,0,2,3:T(4,128)(4,1)S(1)} %copy-done.23, ...), kind=kLoop, calls=%fused_computation.27 | loop fusion | flops 6279168 | bytes 6341120 | tf_op jit(solution)/shard_map/reduce_sum | solution.py:92
  322.3 8.6 %convert_reduce_fusion.1 = (f32[64]{0:T(128)S(1)}, bf16[8192,64]{0,1:T(8,128)(2,1)S(1)}) fusion(bf16[8192,8]{0,1:T(8,128)(2,1)S(1)} %get-tuple-element.187, f32[64]{0:T(128)S(1)} %sub.799, bf16[8192,768]{1,0:T(8,128)(2,1)} %param.3, bf16[768,8,8]{0,1,2:T(8,128)(2,1)S(1)} %convert_bitcast_fusion.2), kind=kOutput, calls=%fused_computation.29 | convolution fusion | flops 807927744 | bytes 13861376 | tf_op jit(solution)/shard_map/dot_general | solution.py:49
  331.1 6.9 %convolution_bitcast_fusion.2 = f32[768,8,8]{0,2,1:T(8,128)S(1)} fusion(bf16[8192,64]{0,1:T(8,128)(2,1)S(1)} %get-tuple-element.202, bf16[8192,768]{1,0:T(8,128)(2,1)} %param.3), kind=kOutput, calls=%fused_computation.33 | convolution fusion | flops 805306368 | bytes 13828096 | tf_op jit(solution)/shard_map/dot_general | solution.py:56
  386.8 15.8 %all-to-all-done.30 = f32[4,16,1,6144]{3,1,2,0:T(8,128)S(1)} async-done(((f32[4,16,1,6144]{3,1,2,0:T(8,128)}), f32[4,16,1,6144]{3,1,2,0:T(8,128)S(1)}, u32[]{:S(2)}, u32[]{:S(2)}) %all-to-all-start.30) | async-done | bytes 1572896 | tf_op jit(solution)/shard_map/all_to_all | solution.py:23
  409.4 12.8 %all-to-all-done.34 = f32[4,16,1,6144]{3,1,2,0:T(8,128)S(1)} async-done(((f32[4,16,1,6144]{3,1,2,0:T(8,128)}), f32[4,16,1,6144]{3,1,2,0:T(8,128)S(1)}, u32[]{:S(2)}, u32[]{:S(2)}) %all-to-all-start.34) | async-done | bytes 1572896 | tf_op jit(solution)/shard_map/all_to_all | solution.py:23
  423.3 10.8 %all-to-all-start.31 = ((f32[2,64,1,6144]{3,1,2,0:T(8,128)}), f32[2,64,1,6144]{3,1,2,0:T(8,128)S(1)}, u32[]{:S(2)}, u32[]{:S(2)}) async-start(f32[2,64,1,6144]{3,1,2,0:T(8,128)} %pad_maximum_fusion.2), calls=%async_computation.31 | async-start | bytes 6291456 | tf_op jit(solution)/shard_map/all_to_all | solution.py:23
  452.0 7.6 %add_reduce_fusion.3 = (f32[6144]{0:T(1024)}, f32[6144]{0:T(1024)}) fusion(f32[4,2,4,4,1,6144]{5,1,0,2,3,4:T(2,128)S(1)} %bitcast.492, f32[4,2,4,4,1,6144]{5,1,0,2,3,4:T(2,128)S(1)} %bitcast.489, pred[4,2,4,4]{1,0,2,3:T(4,128)(4,1)S(1)} %copy-done.20, pred[4,2,4,4]{1,0,2,3:T(4,128)(4,1)S(1)} %copy-done.16, pred[4,2,4,4]{1,0,2,3:T(4,128)(4,1)S(1)} %copy-done.24, ...), kind=kLoop, calls=%fused_computation.25 | loop fusion | flops 6279168 | bytes 6341120 | tf_op jit(solution)/shard_map/reduce_sum | solution.py:92
  467.4 8.6 %convert_reduce_fusion = (f32[64]{0:T(128)S(1)}, bf16[8192,64]{0,1:T(8,128)(2,1)S(1)}) fusion(bf16[8192,8]{0,1:T(8,128)(2,1)S(1)} %get-tuple-element.187, f32[64]{0:T(128)S(1)} %sub.859, bf16[8192,768]{1,0:T(8,128)(2,1)} %param.3, bf16[768,8,8]{0,1,2:T(8,128)(2,1)S(1)} %convert_bitcast_fusion.1), kind=kOutput, calls=%fused_computation.28 | convolution fusion | flops 807927744 | bytes 13861376 | tf_op jit(solution)/shard_map/dot_general | solution.py:49
  476.2 6.9 %convolution_bitcast_fusion.1 = f32[768,8,8]{0,2,1:T(8,128)S(1)} fusion(bf16[8192,64]{0,1:T(8,128)(2,1)S(1)} %get-tuple-element.204, bf16[8192,768]{1,0:T(8,128)(2,1)} %param.3), kind=kOutput, calls=%fused_computation.32 | convolution fusion | flops 805306368 | bytes 13828096 | tf_op jit(solution)/shard_map/dot_general | solution.py:56
  531.3 15.8 %all-to-all-done.38 = f32[4,16,1,6144]{3,1,2,0:T(8,128)S(1)} async-done(((f32[4,16,1,6144]{3,1,2,0:T(8,128)}), f32[4,16,1,6144]{3,1,2,0:T(8,128)S(1)}, u32[]{:S(2)}, u32[]{:S(2)}) %all-to-all-start.38) | async-done | bytes 1572896 | tf_op jit(solution)/shard_map/all_to_all | solution.py:23
  553.8 12.8 %all-to-all-done.42 = f32[4,16,1,6144]{3,1,2,0:T(8,128)S(1)} async-done(((f32[4,16,1,6144]{3,1,2,0:T(8,128)}), f32[4,16,1,6144]{3,1,2,0:T(8,128)S(1)}, u32[]{:S(2)}, u32[]{:S(2)}) %all-to-all-start.42) | async-done | bytes 1572896 | tf_op jit(solution)/shard_map/all_to_all | solution.py:23
  567.7 10.8 %all-to-all-start.39 = ((f32[2,64,1,6144]{3,1,2,0:T(8,128)}), f32[2,64,1,6144]{3,1,2,0:T(8,128)S(1)}, u32[]{:S(2)}, u32[]{:S(2)}) async-start(f32[2,64,1,6144]{3,1,2,0:T(8,128)} %pad_maximum_fusion.4), calls=%async_computation.39 | async-start | bytes 6291456 | tf_op jit(solution)/shard_map/all_to_all | solution.py:23
  596.4 7.2 %add_reduce_fusion.1 = (f32[6144]{0:T(1024)S(1)}, f32[6144]{0:T(1024)S(1)}) fusion(f32[4,2,4,4,1,6144]{5,1,0,2,3,4:T(2,128)S(1)} %bitcast.490, f32[4,2,4,4,1,6144]{5,1,0,2,3,4:T(2,128)S(1)} %bitcast.487, pred[4,2,4,4]{1,0,2,3:T(4,128)(4,1)S(1)} %copy-done.21, pred[4,2,4,4]{1,0,2,3:T(4,128)(4,1)S(1)} %copy-done.17, pred[4,2,4,4]{1,0,2,3:T(4,128)(4,1)S(1)} %copy-done.25, ...), kind=kLoop, calls=%fused_computation.23 | loop fusion | flops 6279168 | bytes 6341120 | tf_op jit(solution)/shard_map/reduce_sum | solution.py:92
  609.3 9.2 %fusion.19 = f32[8192,8]{0,1:T(8,128)} fusion(bf16[8192,768]{1,0:T(8,128)(2,1)} %param.3, f32[8192,8]{0,1:T(8,128)S(1)} %copy-done.6, f32[8,8]{1,0:T(8,128)S(1)} %bitcast.517, bf16[768,8,8]{0,1,2:T(8,128)(2,1)S(1)} %convert_bitcast_fusion), kind=kOutput, calls=%fused_computation.31 | convolution fusion | flops 806813696 | bytes 13205760 | tf_op jit(solution)/shard_map/dot_general | solution.py:49
  (409 shorter events, 373.7 us)
Async XLA Ops:
  6.0 12.7 %all-to-all-start.16 = ((f32[4,1,1,1]{3,2,1,0:T(1,128)}), f32[4,1,1,1]{3,2,1,0:T(1,128)S(1)}, u32[]{:S(2)}, u32[]{:S(2)}) async-start(f32[4,1,1,1]{3,2,1,0:T(1,128)} %stack.214), calls=%async_computation.16 | async-start | bytes 4096 | tf_op jit(solution)/shard_map/all_to_all | solution.py:23
  61.1 9.1 %all-to-all-start.18 = ((f32[4,16,1,1]{1,3,2,0:T(1,128)}), f32[4,16,1,1]{1,3,2,0:T(1,128)S(1)}, u32[]{:S(2)}, u32[]{:S(2)}) async-start(f32[4,16,1,1]{1,3,2,0:T(1,128)} %stack.216), calls=%async_computation.18 | async-start | bytes 4096 | tf_op jit(solution)/shard_map/all_to_all | solution.py:23
  86.0 15.4 %all-to-all-start.19 = ((f32[2,64,1,1]{1,3,2,0:T(1,128)}), f32[2,64,1,1]{1,3,2,0:T(1,128)S(1)}, u32[]{:S(2)}, u32[]{:S(2)}) async-start(f32[2,64,1,1]{1,3,2,0:T(1,128)} %pad_maximum_fusion.10), calls=%async_computation.19 | async-start | bytes 2048 | tf_op jit(solution)/shard_map/all_to_all | solution.py:23
  158.9 11.3 %all-to-all-start.11 = ((f32[2,64,1,768]{3,1,2,0:T(8,128)}), f32[2,64,1,768]{3,1,2,0:T(8,128)S(1)}, u32[]{:S(2)}, u32[]{:S(2)}) async-start(f32[2,64,1,768]{3,1,2,0:T(8,128)} %pad_maximum_fusion.7), calls=%async_computation.11 | async-start | bytes 786432 | tf_op jit(solution)/shard_map/all_to_all | solution.py:23
  198.0 8.8 %all-to-all-start.20 = ((f32[4,1,1,6144]{3,2,1,0:T(1,128)}), f32[4,1,1,6144]{3,2,1,0:T(1,128)}, u32[]{:S(2)}, u32[]{:S(2)}) async-start(f32[4,1,1,6144]{3,2,1,0:T(1,128)} %stack.218), calls=%async_computation.20 | async-start | bytes 196608 | tf_op jit(solution)/shard_map/all_to_all | solution.py:23
  216.2 10.3 %all-to-all-start.21 = ((f32[4,4,1,6144]{3,1,2,0:T(4,128)}), f32[4,4,1,6144]{3,1,2,0:T(4,128)S(1)}, u32[]{:S(2)}, u32[]{:S(2)}) async-start(f32[4,4,1,6144]{3,1,2,0:T(4,128)} %stack.219), calls=%async_computation.21 | async-start | bytes 786432 | tf_op jit(solution)/shard_map/all_to_all | solution.py:23
  227.3 9.7 %all-to-all-start.25 = ((f32[4,4,1,6144]{3,1,2,0:T(4,128)}), f32[4,4,1,6144]{3,1,2,0:T(4,128)S(1)}, u32[]{:S(2)}, u32[]{:S(2)}) async-start(f32[4,4,1,6144]{3,1,2,0:T(4,128)} %stack.223), calls=%async_computation.25 | async-start | bytes 786432 | tf_op jit(solution)/shard_map/all_to_all | solution.py:23
  238.2 18.8 %all-to-all-start.22 = ((f32[4,16,1,6144]{3,1,2,0:T(8,128)}), f32[4,16,1,6144]{3,1,2,0:T(8,128)S(1)}, u32[]{:S(2)}, u32[]{:S(2)}) async-start(f32[4,16,1,6144]{3,1,2,0:T(8,128)} %stack.220), calls=%async_computation.22 | async-start | bytes 3145728 | tf_op jit(solution)/shard_map/all_to_all | solution.py:23
  258.3 17.6 %all-to-all-start.26 = ((f32[4,16,1,6144]{3,1,2,0:T(8,128)}), f32[4,16,1,6144]{3,1,2,0:T(8,128)S(1)}, u32[]{:S(2)}, u32[]{:S(2)}) async-start(f32[4,16,1,6144]{3,1,2,0:T(8,128)} %stack.224), calls=%async_computation.26 | async-start | bytes 3145728 | tf_op jit(solution)/shard_map/all_to_all | solution.py:23
  277.1 15.4 %all-to-all-start.23 = ((f32[2,64,1,6144]{3,1,2,0:T(8,128)}), f32[2,64,1,6144]{3,1,2,0:T(8,128)S(1)}, u32[]{:S(2)}, u32[]{:S(2)}) async-start(f32[2,64,1,6144]{3,1,2,0:T(8,128)} %pad_maximum_fusion), calls=%async_computation.23 | async-start | bytes 6291456 | tf_op jit(solution)/shard_map/all_to_all | solution.py:23
  292.5 9.4 %all-to-all-start.27 = ((f32[2,64,1,6144]{3,1,2,0:T(8,128)}), f32[2,64,1,6144]{3,1,2,0:T(8,128)}, u32[]{:S(2)}, u32[]{:S(2)}) async-start(f32[2,64,1,6144]{3,1,2,0:T(8,128)} %pad_maximum_fusion.1), calls=%async_computation.27 | async-start | bytes 6291456 | tf_op jit(solution)/shard_map/all_to_all | solution.py:23
  343.5 8.7 %all-to-all-start.28 = ((f32[4,1,1,6144]{3,2,1,0:T(1,128)}), f32[4,1,1,6144]{3,2,1,0:T(1,128)}, u32[]{:S(2)}, u32[]{:S(2)}) async-start(f32[4,1,1,6144]{3,2,1,0:T(1,128)} %stack.227), calls=%async_computation.28 | async-start | bytes 196608 | tf_op jit(solution)/shard_map/all_to_all | solution.py:23
  361.6 9.7 %all-to-all-start.29 = ((f32[4,4,1,6144]{3,1,2,0:T(4,128)}), f32[4,4,1,6144]{3,1,2,0:T(4,128)S(1)}, u32[]{:S(2)}, u32[]{:S(2)}) async-start(f32[4,4,1,6144]{3,1,2,0:T(4,128)} %stack.228), calls=%async_computation.29 | async-start | bytes 786432 | tf_op jit(solution)/shard_map/all_to_all | solution.py:23
  372.0 9.7 %all-to-all-start.33 = ((f32[4,4,1,6144]{3,1,2,0:T(4,128)}), f32[4,4,1,6144]{3,1,2,0:T(4,128)S(1)}, u32[]{:S(2)}, u32[]{:S(2)}) async-start(f32[4,4,1,6144]{3,1,2,0:T(4,128)} %stack.232), calls=%async_computation.33 | async-start | bytes 786432 | tf_op jit(solution)/shard_map/all_to_all | solution.py:23
  383.0 19.6 %all-to-all-start.30 = ((f32[4,16,1,6144]{3,1,2,0:T(8,128)}), f32[4,16,1,6144]{3,1,2,0:T(8,128)S(1)}, u32[]{:S(2)}, u32[]{:S(2)}) async-start(f32[4,16,1,6144]{3,1,2,0:T(8,128)} %stack.229), calls=%async_computation.30 | async-start | bytes 3145728 | tf_op jit(solution)/shard_map/all_to_all | solution.py:23
  403.9 18.3 %all-to-all-start.34 = ((f32[4,16,1,6144]{3,1,2,0:T(8,128)}), f32[4,16,1,6144]{3,1,2,0:T(8,128)S(1)}, u32[]{:S(2)}, u32[]{:S(2)}) async-start(f32[4,16,1,6144]{3,1,2,0:T(8,128)} %stack.233), calls=%async_computation.34 | async-start | bytes 3145728 | tf_op jit(solution)/shard_map/all_to_all | solution.py:23
  423.3 14.7 %all-to-all-start.31 = ((f32[2,64,1,6144]{3,1,2,0:T(8,128)}), f32[2,64,1,6144]{3,1,2,0:T(8,128)S(1)}, u32[]{:S(2)}, u32[]{:S(2)}) async-start(f32[2,64,1,6144]{3,1,2,0:T(8,128)} %pad_maximum_fusion.2), calls=%async_computation.31 | async-start | bytes 6291456 | tf_op jit(solution)/shard_map/all_to_all | solution.py:23
  438.1 9.4 %all-to-all-start.35 = ((f32[2,64,1,6144]{3,1,2,0:T(8,128)}), f32[2,64,1,6144]{3,1,2,0:T(8,128)}, u32[]{:S(2)}, u32[]{:S(2)}) async-start(f32[2,64,1,6144]{3,1,2,0:T(8,128)} %pad_maximum_fusion.3), calls=%async_computation.35 | async-start | bytes 6291456 | tf_op jit(solution)/shard_map/all_to_all | solution.py:23
  506.0 9.7 %all-to-all-start.37 = ((f32[4,4,1,6144]{3,1,2,0:T(4,128)}), f32[4,4,1,6144]{3,1,2,0:T(4,128)S(1)}, u32[]{:S(2)}, u32[]{:S(2)}) async-start(f32[4,4,1,6144]{3,1,2,0:T(4,128)} %stack.237), calls=%async_computation.37 | async-start | bytes 786432 | tf_op jit(solution)/shard_map/all_to_all | solution.py:23
  516.4 9.7 %all-to-all-start.41 = ((f32[4,4,1,6144]{3,1,2,0:T(4,128)}), f32[4,4,1,6144]{3,1,2,0:T(4,128)S(1)}, u32[]{:S(2)}, u32[]{:S(2)}) async-start(f32[4,4,1,6144]{3,1,2,0:T(4,128)} %stack.241), calls=%async_computation.41 | async-start | bytes 786432 | tf_op jit(solution)/shard_map/all_to_all | solution.py:23
  527.3 19.7 %all-to-all-start.38 = ((f32[4,16,1,6144]{3,1,2,0:T(8,128)}), f32[4,16,1,6144]{3,1,2,0:T(8,128)S(1)}, u32[]{:S(2)}, u32[]{:S(2)}) async-start(f32[4,16,1,6144]{3,1,2,0:T(8,128)} %stack.238), calls=%async_computation.38 | async-start | bytes 3145728 | tf_op jit(solution)/shard_map/all_to_all | solution.py:23
  548.3 18.3 %all-to-all-start.42 = ((f32[4,16,1,6144]{3,1,2,0:T(8,128)}), f32[4,16,1,6144]{3,1,2,0:T(8,128)S(1)}, u32[]{:S(2)}, u32[]{:S(2)}) async-start(f32[4,16,1,6144]{3,1,2,0:T(8,128)} %stack.242), calls=%async_computation.42 | async-start | bytes 3145728 | tf_op jit(solution)/shard_map/all_to_all | solution.py:23
  567.7 14.7 %all-to-all-start.39 = ((f32[2,64,1,6144]{3,1,2,0:T(8,128)}), f32[2,64,1,6144]{3,1,2,0:T(8,128)S(1)}, u32[]{:S(2)}, u32[]{:S(2)}) async-start(f32[2,64,1,6144]{3,1,2,0:T(8,128)} %pad_maximum_fusion.4), calls=%async_computation.39 | async-start | bytes 6291456 | tf_op jit(solution)/shard_map/all_to_all | solution.py:23
  582.5 9.4 %all-to-all-start.43 = ((f32[2,64,1,6144]{3,1,2,0:T(8,128)}), f32[2,64,1,6144]{3,1,2,0:T(8,128)}, u32[]{:S(2)}, u32[]{:S(2)}) async-start(f32[2,64,1,6144]{3,1,2,0:T(8,128)} %pad_maximum_fusion.5), calls=%async_computation.43 | async-start | bytes 6291456 | tf_op jit(solution)/shard_map/all_to_all | solution.py:23
  (53 other events, 565.1 us)
